TPU v7x, 32 devices: a whole 2x2x4 slice. The times are simulated.
32 devices in a mesh: wide: 8 (over y, x, core), narrow: 4 (over z).
Axes of the slice: x: 2, y: 2, z: 4, core: 2. Of those that a mesh axis runs over, the one named last changes fastest.
Arguments:
- hidden_in: bfloat16 [4096, 1536], P('wide'), may hold values from -64 to 64
- segment_ids: int32 [4096], P('wide'), may hold values from 0 to 7, as said below
- seg_lengths: int32 [8], replicated, may hold values from 1 to 2048, as said below
- seg_offsets: int32 [8], replicated, may hold values from 0 to 4095, as said below
- block_table: int32 [8, 16], replicated, may hold values from -1 to 39, as said below
- attn_gain: bfloat16 [1536], replicated, may hold values from 0.099609375 to 1.8984375
- w_query: bfloat16 [1536, 1536], P('wide', 'narrow'), may hold values from -0.15625 to 0.15625
- b_query: bfloat16 [1536], P('narrow'), may hold values from -128 to 128
- w_keyval: bfloat16 [1536, 512], P('wide'), may hold values from -0.15625 to 0.15625
- b_keyval: bfloat16 [512], replicated, may hold values from -128 to 128
- w_out: bfloat16 [1536, 1536], P('narrow', 'wide'), may hold values from -0.15625 to 0.15625
- mlp_gain: bfloat16 [1536], replicated, may hold values from 0.099609375 to 1.8984375
- w_gate: bfloat16 [1536, 8960], P('wide', 'narrow'), may hold values from -0.15625 to 0.15625
- w_up: bfloat16 [1536, 8960], P('wide', 'narrow'), may hold values from -0.15625 to 0.15625
- w_down: bfloat16 [8960, 1536], P('narrow', 'wide'), may hold values from -0.0625 to 0.0625
- next_gain: bfloat16 [1536], replicated, may hold values from 0.099609375 to 1.8984375
- w_query2: bfloat16 [1536, 1536], P('wide', 'narrow'), may hold values from -0.15625 to 0.15625
- b_query2: bfloat16 [1536], P('narrow'), may hold values from -3 to 3
- w_keyval2: bfloat16 [1536, 512], P('wide'), may hold values from -0.15625 to 0.15625
- b_keyval2: bfloat16 [512], replicated, may hold values from -3 to 3
Outputs:
- hidden_out: bfloat16 [4096, 1536], P('wide')
- next_query: bfloat16 [4096, 1536], P('wide', 'narrow')
- next_keyval: bfloat16 [4096, 512], P('wide', 'narrow')
- kv_cache: bfloat16 [4, 40, 128, 128], P('narrow', 'wide')
Inputs may be any that keep to these rules, and one draw needn't show every extreme that they name: `segment_ids`: segment s covers tokens seg_offsets[s] to seg_offsets[s] + seg_lengths[s] - 1. `seg_lengths`: they sum to 4096. seg_offsets[0] = 0 and seg_offsets[s + 1] = seg_offsets[s] + seg_lengths[s]. `block_table`: entry j of row s is a page for j below ceil(seg_lengths[s] / 128) and -1 beyond; no page appears twice.
All inputs are finite; a program needn't handle non-finite values.
Results may differ from a plain program's by a relative error of at most 0.017.
Values may be sent and summed in bfloat16 or wider, within the bound.
No kernel may reach another device: no remote copies, remote signals or barrier semaphores. Data moves between devices by JAX's collectives and lax.ppermute only.
A program may use at most 128 MiB of HBM per device.

v0:
```python
import math
import jax
import jax.numpy as jnp
from jax import lax
from jax.sharding import PartitionSpec as P

HD = 128
PAGE_LEN = 128
norm_eps = 1e-06
rope_base = 1000000.0
masked_score = -1e30


def rms_norm(activations, gain_vector):
    values = activations.astype(jnp.float32)
    row_scale = lax.rsqrt(jnp.mean(values * values, axis=-1, keepdims=True) + norm_eps)
    return (values * row_scale * gain_vector.astype(jnp.float32)).astype(jnp.bfloat16)


def rotate(values, positions):
    half_dim = values.shape[-1] // 2
    frequency = rope_base ** (-(jnp.arange(half_dim, dtype=jnp.float32) * 2.0 / values.shape[-1]))
    angles = positions.astype(jnp.float32)[:, None, None] * frequency
    cosine = jnp.cos(angles)
    sine_part = jnp.sin(angles)
    lower_half = values[..., :half_dim]
    upper_half = values[..., half_dim:]
    return jnp.concatenate(
        [
            lower_half * cosine - upper_half * sine_part,
            upper_half * cosine + lower_half * sine_part,
        ],
        axis=-1,
    )


def lookup(table, indices):
    table_match = indices[..., None] == jnp.arange(table.shape[0], dtype=jnp.int32)
    return jnp.sum(jnp.where(table_match, table, 0), axis=-1)


def fold_rows(normed, first_weight, second_weight):
    return (
        jnp.dot(
            normed,
            lax.all_gather(first_weight, "wide", axis=0, tiled=True),
            preferred_element_type=jnp.float32,
        ),
        jnp.dot(
            normed,
            lax.all_gather(second_weight, "wide", axis=0, tiled=True),
            preferred_element_type=jnp.float32,
        ),
    )


def column_terms(left_rows, weight_block):
    return jnp.dot(
        left_rows,
        lax.all_gather(weight_block, "wide", axis=1, tiled=True),
        preferred_element_type=jnp.float32,
    )


def keyval_block(w_keyval, b_keyval, head_pair):
    pair_width = 2 * HD
    pair_offset = head_pair * pair_width
    return (w_keyval, b_keyval, pair_offset)


def add_branch(partial_terms, base_rows, narrow_index):
    share_sum = lax.psum_scatter(
        partial_terms.astype(jnp.bfloat16), "narrow", scatter_dimension=1, tiled=True
    ).astype(jnp.float32)
    share_width = share_sum.shape[1]
    base_share = lax.dynamic_slice_in_dim(base_rows, narrow_index * share_width, share_width, 1)
    updated = (base_share.astype(jnp.float32) + share_sum).astype(jnp.bfloat16)
    result_rows = lax.all_gather(updated, "narrow", axis=1, tiled=True)
    return result_rows


def attend(queries, keys_all, values_all, segment_ids, seg_offsets, row_base):
    tok_rows = queries.shape[0]
    local_heads = queries.shape[1] // HD
    total_rows = keys_all.shape[0]
    key_block = math.gcd(total_rows, 512)
    score_scale = HD ** (-0.5)
    stacked = (
        queries.reshape(tok_rows, local_heads, HD)
        .transpose(1, 0, 2)
        .reshape(local_heads * tok_rows, HD)
    )
    query_pos = row_base + jnp.arange(tok_rows, dtype=jnp.int32)
    query_pos_all = jnp.tile(query_pos, local_heads)
    query_seg_all = jnp.tile(segment_ids, local_heads)
    lowest = lookup(seg_offsets, segment_ids[:1])[0]
    first_block = lowest // key_block
    last_block = (row_base + tok_rows - 1) // key_block

    def visit_block(block_number, state_now):
        running_max, running_sum, accumulated = state_now
        key_start = block_number * key_block
        keys_here = lax.dynamic_slice_in_dim(keys_all, key_start, key_block, 0)
        values_here = lax.dynamic_slice_in_dim(values_all, key_start, key_block, 0)
        key_pos = key_start + jnp.arange(key_block, dtype=jnp.int32)
        key_seg = jnp.sum((key_pos[:, None] >= seg_offsets[None, 1:]).astype(jnp.int32), axis=1)
        visible = (
            (key_seg[None, :] == query_seg_all[:, None])
            & (key_pos[None, :] <= query_pos_all[:, None])
            & (key_pos[None, :] >= 0)
        )
        scores = (
            jnp.einsum("qd,kd->qk", stacked, keys_here, preferred_element_type=jnp.float32)
            * score_scale
        )
        scores = jnp.where(visible, scores, masked_score)
        new_max = jnp.maximum(running_max, jnp.max(scores, axis=1))
        weights = jnp.where(visible, jnp.exp(scores - new_max[:, None]), 0.0)
        factor = jnp.exp(running_max - new_max)
        running_sum = running_sum * factor + jnp.sum(weights, axis=1)
        accumulated = accumulated * factor[:, None] + jnp.dot(
            weights.astype(jnp.bfloat16), values_here, preferred_element_type=jnp.float32
        )
        return (new_max, running_sum, accumulated)

    row_count = stacked.shape[0]
    initial = (
        jnp.full((row_count,), masked_score, jnp.float32),
        jnp.zeros((row_count,), jnp.float32),
        jnp.zeros((row_count, HD), jnp.float32),
    )
    final_max, final_sum, accumulated = lax.fori_loop(
        first_block, last_block + 1, visit_block, initial
    )
    mixed_heads = (
        (accumulated / final_sum[:, None]).reshape(local_heads, tok_rows, HD).transpose(1, 0, 2)
    )
    return mixed_heads.reshape(tok_rows, local_heads * HD).astype(jnp.bfloat16)


def fill_pages(source, seg_lengths, seg_offsets, block_table, first_page, page_count):
    pages_here = first_page + jnp.arange(page_count, dtype=jnp.int32)
    page_match = block_table[None, :, :] == pages_here[:, None, None]
    seg_grid = jnp.arange(block_table.shape[0], dtype=jnp.int32)[None, :, None]
    page_grid = jnp.arange(block_table.shape[1], dtype=jnp.int32)[None, None, :]
    page_owner = jnp.sum(jnp.where(page_match, seg_grid, 0), axis=(1, 2))
    logical = jnp.sum(jnp.where(page_match, page_grid, 0), axis=(1, 2))
    in_use = jnp.any(page_match, axis=(1, 2))
    first_token = lookup(seg_offsets, page_owner) + logical * PAGE_LEN
    filled = lookup(seg_lengths, page_owner) - logical * PAGE_LEN
    slot_index = jnp.arange(PAGE_LEN, dtype=jnp.int32)
    row_ids = jnp.clip(first_token[:, None] + slot_index[None, :], 0, source.shape[0] - 1)
    keep_slot = in_use[:, None] & (slot_index[None, :] < filled[:, None])
    taken_rows = jnp.take(source, row_ids.reshape(-1), axis=0).reshape(
        page_count, PAGE_LEN, source.shape[1]
    )
    return jnp.where(keep_slot[:, :, None], taken_rows, jnp.zeros((), source.dtype))


def local(
    hidden_in,
    segment_ids,
    seg_lengths,
    seg_offsets,
    block_table,
    attn_gain,
    w_query,
    b_query,
    w_keyval,
    b_keyval,
    w_out,
    mlp_gain,
    w_gate,
    w_up,
    w_down,
    next_gain,
    w_query2,
    b_query2,
    w_keyval2,
    b_keyval2,
):
    tok_rows = hidden_in.shape[0]
    wide_index = lax.axis_index("wide")
    narrow_index = lax.axis_index("narrow")
    head_pair = narrow_index // 2
    kind_index = narrow_index % 2
    row_base = wide_index * tok_rows
    positions = row_base + jnp.arange(tok_rows, dtype=jnp.int32) - lookup(seg_offsets, segment_ids)
    normed = rms_norm(hidden_in, attn_gain)
    kv_weight, kv_bias, pair_offset = keyval_block(w_keyval, b_keyval, head_pair)
    query_sum, keyval_sum = fold_rows(normed, w_query, kv_weight)
    queries = query_sum + b_query.astype(jnp.float32)
    local_heads = queries.shape[1] // HD
    queries = (
        rotate(queries.reshape(tok_rows, local_heads, HD), positions)
        .reshape(tok_rows, local_heads * HD)
        .astype(jnp.bfloat16)
    )
    keyvals = (keyval_sum + kv_bias.astype(jnp.float32)).reshape(tok_rows, -1, 2, HD)
    keyvals = jnp.stack([rotate(keyvals[:, :, 0, :], positions), keyvals[:, :, 1, :]], axis=2)
    keyvals = keyvals.reshape(tok_rows, kv_weight.shape[1]).astype(jnp.bfloat16)
    gathered = lax.all_gather(keyvals, "wide", axis=0, tiled=True)
    source = lax.dynamic_slice_in_dim(gathered, pair_offset + kind_index * HD, HD, 1)
    keys_all = lax.dynamic_slice_in_dim(gathered, pair_offset, HD, 1)
    values_all = lax.dynamic_slice_in_dim(gathered, pair_offset + HD, HD, 1)
    mixed_heads = attend(queries, keys_all, values_all, segment_ids, seg_offsets, row_base)
    residual = add_branch(column_terms(mixed_heads, w_out), hidden_in, narrow_index)
    normed_mlp = rms_norm(residual, mlp_gain)
    gate_sum, up_sum = fold_rows(normed_mlp, w_gate, w_up)
    hidden_units = (jax.nn.silu(gate_sum) * up_sum).astype(jnp.bfloat16)
    hidden_out = add_branch(column_terms(hidden_units, w_down), residual, narrow_index)
    normed_next = rms_norm(hidden_out, next_gain)
    kv_weight_next, kv_bias_next, pair_offset_next = keyval_block(w_keyval2, b_keyval2, head_pair)
    query_next, keyval_next = fold_rows(normed_next, w_query2, kv_weight_next)
    next_query = (query_next + b_query2.astype(jnp.float32)).astype(jnp.bfloat16)
    keyval_next = keyval_next + kv_bias_next.astype(jnp.float32)
    next_keyval = lax.dynamic_slice_in_dim(
        keyval_next, pair_offset_next + kind_index * HD, HD, 1
    ).astype(jnp.bfloat16)
    page_count = tok_rows // PAGE_LEN + 1
    cache_block = fill_pages(
        source, seg_lengths, seg_offsets, block_table, wide_index * page_count, page_count
    )
    return (hidden_out, next_query, next_keyval, cache_block[None])


def solution(mesh):
    placed = (
        P("wide", None),
        P("wide"),
        P(),
        P(),
        P(),
        P(),
        P("wide", "narrow"),
        P("narrow"),
        P("wide", None),
        P(),
        P("narrow", "wide"),
        P(),
        P("wide", "narrow"),
        P("wide", "narrow"),
        P("narrow", "wide"),
        P(),
        P("wide", "narrow"),
        P("narrow"),
        P("wide", None),
        P(),
    )
    return jax.shard_map(
        local,
        mesh=mesh,
        in_specs=placed,
        out_specs=(
            P("wide", None),
            P("wide", "narrow"),
            P("wide", "narrow"),
            P("narrow", "wide", None, None),
        ),
        check_vma=False,
    )
```

profile of v0, /device:TPU:0, one launch (start us, length us, event | category | flops | bytes accessed | tf_op | source)
XLA Modules:
  0.0 521.2 jit_solution(14658357420002267087)
XLA Ops:
  7.2 0.7 all-gather.12.cloned.1.call-update
  7.9 0.7 all-gather.16.cloned.1.call-update
  8.7 0.7 convert_element_type.106
  9.4 0.7 convert_element_type.108
  10.1 0.8 select_reduce_fusion
  10.9 1.8 fusion.17
  12.7 0.5 multiply_cosine_fusion
  13.2 25.1 %all-gather.12.cloned.1.call-done = bf16[1536,512]{1,0:T(8,128)(2,1)} async-done(((bf16[192,512]{1,0:T(8,128)(2,1)}), bf16[1536,512]{1,0:T(8,128)(2,1)}) %all-gather.12.cloned.1.call-update) | async-done | bytes 1572880 | tf_op jit(solution)/shard_map/all_gather | solution.py:51
  38.3 3.0 convolution_add_fusion.1
  41.4 0.1 subtract_convert_fusion.1
  41.6 1.0 copy.42
  42.7 0.5 all-gather.18.cloned.1.call-update
  43.3 0.5 slice.25
  43.8 1.3 fusion.44
  47.8 16.5 %all-gather.16.cloned.1.call-done = bf16[1536,384]{1,0:T(8,128)(2,1)} async-done(((bf16[192,384]{1,0:T(8,128)(2,1)}), bf16[1536,384]{1,0:T(8,128)(2,1)}) %all-gather.16.cloned.1.call-update) | async-done | bytes 1179664 | tf_op jit(solution)/shard_map/all_gather | solution.py:46
  64.3 2.2 convolution_add_fusion.3
  66.5 0.1 subtract_convert_fusion
  66.7 0.2 copy.40
  66.9 36.6 %all-gather.14.cloned.1.call-done = bf16[4096,512]{1,0:T(8,128)(2,1)} async-done(((bf16[512,512]{1,0:T(8,128)(2,1)}), bf16[4096,512]{1,0:T(8,128)(2,1)}) %all-gather.14.cloned.1.call-update) | async-done | bytes 4194320 | tf_op jit(solution)/shard_map/all_gather | solution.py:202
  103.5 3.1 constant_dynamic-slice_fusion
  106.6 5.7 %while.15 = (s32[]{:T(128)}, f32[1536]{0:T(1024)S(1)}, f32[1536]{0:T(1024)S(1)}, f32[1536,128]{1,0:T(8,128)S(1)}, s32[]{:T(128)}, /*index=5*/s32[8]{0:T(128)S(1)...) while((s32[]{:T(128)}, f32[1536]{0:T(1024)S(1)}, ...), condition=%wide.region_7.8_spmd.clone, body=%wide.region_3.7_spmd.clone.sunk | while | flops 419576320 | bytes 11870495 | solution.py:132
  106.8 0.1 convert_reduce_fusion.2
  106.9 2.2 fusion.73
  109.1 1.4 fusion.74
  110.5 1.8 convolution_add_fusion.5
  112.4 0.3 divide_convert_fusion
  112.7 0.2 copy.41
  112.8 16.5 %all-gather.18.cloned.1.call-done = bf16[384,1536]{0,1:T(8,128)(2,1)} async-done(((bf16[384,192]{0,1:T(8,128)(2,1)}), bf16[384,1536]{0,1:T(8,128)(2,1)}) %all-gather.18.cloned.1.call-update) | async-done | bytes 1179664 | tf_op jit(solution)/shard_map/all_gather | solution.py:60
  129.3 2.3 convolution_convert_fusion.1
  131.6 1.6 copy.43
  133.3 41.8 %reduce-scatter.7.cloned.1.call-done = bf16[384,512]{1,0:T(8,128)(2,1)} async-done(((bf16[1536,512]{1,0:T(8,128)(2,1)}), bf16[384,512]{1,0:T(8,128)(2,1)}) %reduce-scatter.7.cloned.1.call-update) | async-done | bytes 393232
  175.1 1.2 copy.44
  176.3 1.8 add_convert_fusion.1
  178.3 0.7 all-gather.22.cloned.1.call-update
  179.0 0.7 all-gather.24.cloned.1.call-update
  179.8 0.7 all-gather.26.cloned.1.call-update
  180.5 0.2 reduce-scatter.9.cloned.1.call-start
  180.7 33.7 %all-gather.20.cloned.1.call-done = bf16[512,1536]{1,0:T(8,128)(2,1)} async-done(((bf16[512,384]{1,0:T(8,128)(2,1)}), bf16[512,1536]{1,0:T(8,128)(2,1)}) %all-gather.20.cloned.1.call-update) | async-done | bytes 1572880 | tf_op jit(solution)/shard_map/all_gather | solution.py:78
  214.4 1.8 fusion.20
  216.2 47.9 %all-gather.22.cloned.1.call-done = bf16[1536,2240]{1,0:T(8,128)(2,1)} async-done(((bf16[192,2240]{1,0:T(8,128)(2,1)}), bf16[1536,2240]{1,0:T(8,128)(2,1)}) %all-gather.22.cloned.1.call-update) | async-done | bytes 6881296 | tf_op jit(solution)/shard_map/all_gather | solution.py:46
  264.2 9.5 %fusion.28 = f32[512,2240]{0,1:T(8,128)} fusion(bf16[1536,2240]{1,0:T(8,128)(2,1)} %all-gather.22.cloned.1.call-done, bf16[512,1536]{1,0:T(8,128)(2,1)} %all-gather.20.cloned.1.call-done, f32[1536]{0:T(1024)S(1)} %convert_element_type.121, f32[512]{0:T(512)S(1)} %add_rsqrt_fusion.1), kind=kOutput, calls=%fused_computation.52 | convolution fusion | flops 3526361088 | bytes 13049856 | tf_op jit(solution)/shard_map/dot_general | solution.py:44
  273.6 41.3 %all-gather.24.cloned.1.call-done = bf16[1536,2240]{1,0:T(8,128)(2,1)} async-done(((bf16[192,2240]{1,0:T(8,128)(2,1)}), bf16[1536,2240]{1,0:T(8,128)(2,1)}) %all-gather.24.cloned.1.call-update) | async-done | bytes 6881296 | tf_op jit(solution)/shard_map/all_gather | solution.py:51
  314.9 50.8 %all-gather.26.cloned.1.call-done = bf16[2240,1536]{0,1:T(8,128)(2,1)} async-done(((bf16[2240,192]{0,1:T(8,128)(2,1)}), bf16[2240,1536]{0,1:T(8,128)(2,1)}) %all-gather.26.cloned.1.call-update) | async-done | bytes 6881296 | tf_op jit(solution)/shard_map/all_gather | solution.py:60
  365.7 15.9 %convolution_convert_fusion = bf16[512,1536]{1,0:T(8,128)(2,1)} fusion(bf16[2240,1536]{0,1:T(8,128)(2,1)} %all-gather.26.cloned.1.call-done, bf16[1536,2240]{1,0:T(8,128)(2,1)} %all-gather.24.cloned.1.call-done, f32[512,2240]{0,1:T(8,128)} %fusion.28, bf16[512,1536]{1,0:T(8,128)(2,1)S(1)} %copy-done.2, f32[1536]{0:T(1024)S(1)} %convert_element_type.121, ...), kind=kOutput, calls=%fused_computation.40 | convolution fusion | flops 7057244160 | bytes 21504000 | tf_op jit(solution)/shard_map/dot_general | solution.py:58
  381.6 2.7 copy.45
  384.4 35.4 %reduce-scatter.9.cloned.1.call-done = bf16[384,512]{1,0:T(8,128)(2,1)} async-done(((bf16[1536,512]{1,0:T(8,128)(2,1)}), bf16[384,512]{1,0:T(8,128)(2,1)}) %reduce-scatter.9.cloned.1.call-update) | async-done | bytes 393232
  419.8 1.2 copy.46
  421.0 0.8 add_convert_fusion
  421.9 0.5 all-gather.32.cloned.1.call-update
  422.5 0.7 all-gather.30.cloned.1.call-update
  423.2 0.3 fusion.37
  423.6 0.2 select_reduce_fusion.2
  424.0 0.3 compare_reduce_fusion
  424.2 0.1 fusion.41
  424.3 2.0 gather_fusion
  426.3 0.9 select_select_fusion
  427.2 30.9 %all-gather.28.cloned.1.call-done = bf16[512,1536]{1,0:T(8,128)(2,1)} async-done(((bf16[512,384]{1,0:T(8,128)(2,1)}), bf16[512,1536]{1,0:T(8,128)(2,1)}) %all-gather.28.cloned.1.call-update) | async-done | bytes 1572880 | tf_op jit(solution)/shard_map/all_gather | solution.py:78
  458.1 1.8 fusion.23
  459.9 24.6 %all-gather.32.cloned.1.call-done = bf16[1536,512]{1,0:T(8,128)(2,1)} async-done(((bf16[192,512]{1,0:T(8,128)(2,1)}), bf16[1536,512]{1,0:T(8,128)(2,1)}) %all-gather.32.cloned.1.call-update) | async-done | bytes 1572880 | tf_op jit(solution)/shard_map/all_gather | solution.py:51
  484.5 2.9 fusion.30
  487.4 0.7 fusion.35
  488.1 22.4 %all-gather.30.cloned.1.call-done = bf16[1536,384]{1,0:T(8,128)(2,1)} async-done(((bf16[192,384]{1,0:T(8,128)(2,1)}), bf16[1536,384]{1,0:T(8,128)(2,1)}) %all-gather.30.cloned.1.call-update) | async-done | bytes 1179664 | tf_op jit(solution)/shard_map/all_gather | solution.py:46
  510.5 3.0 fusion.26
  513.5 1.1 copy.63
  (75 shorter events, 1.2 us)
Async XLA Ops:
  7.2 31.1 %all-gather.12.cloned.1.call-start = ((), (), s32[]{:S(2)}) async-start(), calls=%async_computation.2 | async-start | bytes 1769472 | tf_op jit(solution)/shard_map/all_gather | solution.py:51
  7.9 56.4 %all-gather.16.cloned.1.call-start = ((), (), s32[]{:S(2)}) async-start(), calls=%async_computation.4 | async-start | bytes 1327104 | tf_op jit(solution)/shard_map/all_gather | solution.py:46
  8.6 94.9 %all-gather.14.cloned.1.call-start = ((), (), s32[]{:S(2)}) async-start(), calls=%async_computation.3 | async-start | bytes 4718592 | tf_op jit(solution)/shard_map/all_gather | solution.py:202
  41.3 2.0 copy-start.3
  41.3 2.5 copy-start.7
  41.3 6.4 %copy-start.8 = (bf16[384]{0:T(512)(128)(2,1)S(1)}, bf16[384]{0:T(512)(128)(2,1)}, u32[]{:S(2)}) copy-start(bf16[384]{0:T(512)(128)(2,1)} %param.29) | copy-start | bytes 2308
  41.3 22.9 %copy-start.1 = (bf16[512,1536]{1,0:T(8,128)(2,1)S(1)}, bf16[512,1536]{1,0:T(8,128)(2,1)}, u32[]{:S(2)}) copy-start(bf16[512,1536]{1,0:T(8,128)(2,1)} %param.22) | copy-start | bytes 4718596
  42.7 86.7 %all-gather.18.cloned.1.call-start = ((), (), s32[]{:S(2)}) async-start(), calls=%async_computation.5 | async-start | bytes 1327104 | tf_op jit(solution)/shard_map/all_gather | solution.py:60
  43.2 131.9 %reduce-scatter.7.cloned.1.call-start = ((), (), s32[]{:S(2)}) async-start(), calls=%async_computation.13 | async-start | bytes 1966080
  133.2 47.5 %copy-start.5 = (bf16[1536]{0:T(1024)(128)(2,1)S(1)}, bf16[1536]{0:T(1024)(128)(2,1)}, u32[]{:S(2)}) copy-start(bf16[1536]{0:T(1024)(128)(2,1)} %param.33) | copy-start | bytes 9220
  133.3 81.2 %all-gather.20.cloned.1.call-start = ((), (), s32[]{:S(2)}) async-start(), calls=%async_computation.6 | async-start | bytes 1966080 | tf_op jit(solution)/shard_map/all_gather | solution.py:78
  178.2 85.9 %all-gather.22.cloned.1.call-start = ((), (), s32[]{:S(2)}) async-start(), calls=%async_computation.7 | async-start | bytes 7962624 | tf_op jit(solution)/shard_map/all_gather | solution.py:46
  179.0 136.0 %all-gather.24.cloned.1.call-start = ((), (), s32[]{:S(2)}) async-start(), calls=%async_computation.8 | async-start | bytes 7962624 | tf_op jit(solution)/shard_map/all_gather | solution.py:51
  179.7 186.0 %all-gather.26.cloned.1.call-start = ((), (), s32[]{:S(2)}) async-start(), calls=%async_computation.9 | async-start | bytes 7962624 | tf_op jit(solution)/shard_map/all_gather | solution.py:60
  180.5 239.3 %reduce-scatter.9.cloned.1.call-start = ((), (), s32[]{:S(2)}) async-start(), calls=%async_computation.14 | async-start | bytes 1966080
  216.2 149.5 %copy-start.2 = (bf16[512,1536]{1,0:T(8,128)(2,1)S(1)}, bf16[512,1536]{1,0:T(8,128)(2,1)}, u32[]{:S(2)}) copy-start(bf16[512,1536]{1,0:T(8,128)(2,1)} %all-gather.20.cloned.1.call-done) | copy-start | bytes 4718596
  381.6 41.6 %copy-start.4 = (s32[8,16]{1,0:T(8,128)S(1)}, s32[8,16]{1,0:T(8,128)}, u32[]{:S(2)}) copy-start(s32[8,16]{1,0:T(8,128)} %param.26) | copy-start | bytes 1540
  381.6 42.0 %copy-start.10 = (s32[8]{0:T(128)S(1)}, s32[8]{0:T(128)}, u32[]{:S(2)}) copy-start(s32[8]{0:T(128)} %param.24) | copy-start | bytes 100
  381.6 42.2 %copy-start.6 = (bf16[1536]{0:T(1024)(128)(2,1)S(1)}, bf16[1536]{0:T(1024)(128)(2,1)}, u32[]{:S(2)}) copy-start(bf16[1536]{0:T(1024)(128)(2,1)} %param.37) | copy-start | bytes 9220
  381.6 42.2 %copy-start.11 = (bf16[512]{0:T(512)(128)(2,1)S(1)}, bf16[512]{0:T(512)(128)(2,1)}, u32[]{:S(2)}) copy-start(bf16[512]{0:T(512)(128)(2,1)} %param.41) | copy-start | bytes 3076
  381.6 42.3 %copy-start.9 = (bf16[384]{0:T(512)(128)(2,1)S(1)}, bf16[384]{0:T(512)(128)(2,1)}, u32[]{:S(2)}) copy-start(bf16[384]{0:T(512)(128)(2,1)} %param.39) | copy-start | bytes 2308
  384.3 73.8 %all-gather.28.cloned.1.call-start = ((), (), s32[]{:S(2)}) async-start(), calls=%async_computation.10 | async-start | bytes 1966080 | tf_op jit(solution)/shard_map/all_gather | solution.py:78
  421.9 62.7 %all-gather.32.cloned.1.call-start = ((), (), s32[]{:S(2)}) async-start(), calls=%async_computation.12 | async-start | bytes 1769472 | tf_op jit(solution)/shard_map/all_gather | solution.py:51
  422.4 88.1 %all-gather.30.cloned.1.call-start = ((), (), s32[]{:S(2)}) async-start(), calls=%async_computation.11 | async-start | bytes 1327104 | tf_op jit(solution)/shard_map/all_gather | solution.py:46
  459.9 50.6 %copy-start = (bf16[512,1536]{1,0:T(8,128)(2,1)S(1)}, bf16[512,1536]{1,0:T(8,128)(2,1)}, u32[]{:S(2)}) copy-start(bf16[512,1536]{1,0:T(8,128)(2,1)} %all-gather.28.cloned.1.call-done) | copy-start | bytes 4718596
Sparse Core Ops, SparseCore 0:
  9.9 28.3 all-gather.11
  40.2 24.0 all-gather.15
  66.8 36.7 all-gather.13
  105.2 24.0 all-gather.17
  133.4 41.7 reduce-scatter.6
  178.3 36.0 all-gather.19
  216.3 47.7 all-gather.21
  266.0 48.8 all-gather.23
  316.8 48.8 all-gather.25
  384.5 35.2 reduce-scatter.8
  422.0 36.0 all-gather.27
  459.8 24.6 all-gather.31
  486.4 24.0 all-gather.29
where the time goes:
time: 522 us; the launch traced here: 521 us
  waiting for transfers between devices  429 us (82%)
  matrix products  42.8 us (8%)
  between operations  16.9 us (3%)
  other arithmetic  16.8 us (3%)
  local copies, waits for them, and re-layouts  15.1 us (3%)
    all_gather x3, waiting for transfers between devices, fold_rows(): lax.all_gather(second_weight, 'wide', axis=0, tiled=True)  91 us
    all_gather x3, waiting for transfers between devices, fold_rows(): lax.all_gather(first_weight, 'wide', axis=0, tiled=True)  86.8 us
    unnamed x15, waiting for transfers between devices  82.5 us
    all_gather x2, waiting for transfers between devices, column_terms(): lax.all_gather(weight_block, 'wide', axis=1, tiled=True)  67.3 us
    all_gather x2, waiting for transfers between devices, add_branch(): result_rows = lax.all_gather(updated, 'narrow', axis=1, tiled=True)  64.6 us
    all_gather x1, waiting for transfers between devices, local(): gathered = lax.all_gather(keyvals, 'wide', axis=0, tiled=True)  36.6 us
    dot_general x2, matrix products, column_terms(): jnp.dot(left_rows, lax.all_gather(weight_block, 'wide', axis=1, tiled=Tru...  18.2 us
    dot_general x3, matrix products, fold_rows(): jnp.dot(normed, lax.all_gather(first_weight, 'wide', axis=0, tiled=True),...  14.7 us
  transfers between devices with their start and end apart: 13, of which 13 were waited for; matrix products, arithmetic and copies ran while one was open for 8% of the time, Pallas kernels for 0%

commit v1 on v0

--- a/solution.py
+++ b/solution.py
@@ -3,12 +3,32 @@
 import jax.numpy as jnp
 from jax import lax
 from jax.sharding import PartitionSpec as P
+from jax.lax import axis_index, axis_size, ppermute
 
 HD = 128
 PAGE_LEN = 128
 norm_eps = 1e-06
 rope_base = 1000000.0
 masked_score = -1e30
+
+
+def push_the_hubs(z, dim_no):
+    all_values = list(z.shape[1:])
+    all_values[dim_no] *= z.shape[0]
+    return jnp.moveaxis(z, 0, dim_no).reshape(all_values)
+
+
+def pair_skins(page, row_axis, on_dim):
+    many = axis_size(row_axis)
+    steps_seen = tuple(((pp, (pp + 1) % many) for pp in range(many)))
+    xs_all = [page]
+    while len(xs_all) < many:
+        block_next = ppermute(xs_all[-1], axis_name=row_axis, perm=steps_seen)
+        xs_all.append(block_next)
+    passed = axis_index(row_axis)
+    mat_out = jnp.stack(xs_all)
+    xs_all = mat_out[(passed - jnp.arange(many)) % many]
+    return push_the_hubs(xs_all, on_dim)
 
 
 def rms_norm(activations, gain_vector):
@@ -56,9 +76,7 @@
 
 def column_terms(left_rows, weight_block):
     return jnp.dot(
-        left_rows,
-        lax.all_gather(weight_block, "wide", axis=1, tiled=True),
-        preferred_element_type=jnp.float32,
+        left_rows, pair_skins(weight_block, "wide", 1), preferred_element_type=jnp.float32
     )
 
 

time: 522 us -> 490 us (0.939)
  waiting for transfers between devices: 429 us -> 380 us
  local copies, waits for them, and re-layouts: 15.1 us -> 31.9 us
    ppermute x0 -> x14, waiting for transfers between devices: none -> 157 us  [pair_skins(): block_next = ppermute(xs_all[-1], axis_name=row_axis, perm=steps_seen)]
    all_gather x2 -> x0, waiting for transfers between devices: 67.3 us -> none  [column_terms(): lax.all_gather(weight_block, 'wide', axis=1, tiled=True)]
    all_gather x3, waiting for transfers between devices: 86.8 us -> 22.4 us  [fold_rows(): lax.all_gather(first_weight, 'wide', axis=0, tiled=True)]
    all_gather x3, waiting for transfers between devices: 91 us -> 53.8 us  [fold_rows(): lax.all_gather(second_weight, 'wide', axis=0, tiled=True)]
    all_gather x2, waiting for transfers between devices: 64.6 us -> 30.9 us  [add_branch(): result_rows = lax.all_gather(updated, 'narrow', axis=1, tiled=True)]
    all_gather x1, waiting for transfers between devices: 36.6 us -> 18 us  [local(): gathered = lax.all_gather(keyvals, 'wide', axis=0, tiled=True)]
    unnamed x15 -> x13, waiting for transfers between devices: 82.5 us -> 97.6 us
    gather x0 -> x2, local copies, waits for them, and re-layouts: none -> 8.2 us  [pair_skins(): xs_all = mat_out[(passed - jnp.arange(many)) % many]]
  transfers between devices with their start and end apart: 13 -> 25, of which waited for: 13 -> 22; matrix products, arithmetic and copies ran while one was open for 8% -> 10% of each run, Pallas kernels for 0% -> 0%
where the time goes in v1:
time: 490 us; the launch traced here: 489 us
  waiting for transfers between devices  380 us (78%)
  matrix products  42.2 us (9%)
  local copies, waits for them, and re-layouts  31.9 us (7%)
  between operations  17 us (3%)
  other arithmetic  16.9 us (3%)
    ppermute x14, waiting for transfers between devices, pair_skins(): block_next = ppermute(xs_all[-1], axis_name=row_axis, perm=steps_seen)  157 us
    unnamed x13, waiting for transfers between devices  97.6 us
    all_gather x3, waiting for transfers between devices, fold_rows(): lax.all_gather(second_weight, 'wide', axis=0, tiled=True)  53.8 us
    all_gather x2, waiting for transfers between devices, add_branch(): result_rows = lax.all_gather(updated, 'narrow', axis=1, tiled=True)  30.9 us
    all_gather x3, waiting for transfers between devices, fold_rows(): lax.all_gather(first_weight, 'wide', axis=0, tiled=True)  22.4 us
    all_gather x1, waiting for transfers between devices, local(): gathered = lax.all_gather(keyvals, 'wide', axis=0, tiled=True)  18 us
    dot_general x2, matrix products, column_terms(): jnp.dot(left_rows, pair_skins(weight_block, 'wide', 1), preferred_element...  16.9 us
    dot_general x3, matrix products, fold_rows(): jnp.dot(normed, lax.all_gather(first_weight, 'wide', axis=0, tiled=True),...  15.3 us
  transfers between devices with their start and end apart: 25, of which 22 were waited for; matrix products, arithmetic and copies ran while one was open for 10% of the time, Pallas kernels for 0%

profile of v1, /device:TPU:0, one launch (start us, length us, event | category | flops | bytes accessed | tf_op | source)
XLA Modules:
  0.0 489.4 jit_solution(898228354492659247)
XLA Ops:
  7.2 0.7 all-gather.10.cloned.1.call-update
  7.9 0.7 all-gather.14.cloned.1.call-update
  8.7 0.7 convert_element_type.106
  10.1 0.8 select_reduce_fusion
  10.9 1.8 fusion.17
  13.2 25.1 %all-gather.10.cloned.1.call-done = bf16[1536,512]{1,0:T(8,128)(2,1)} async-done(((bf16[192,512]{1,0:T(8,128)(2,1)}), bf16[1536,512]{1,0:T(8,128)(2,1)}) %all-gather.10.cloned.1.call-update) | async-done | bytes 1572880 | tf_op jit(solution)/shard_map/all_gather | solution.py:71
  38.3 3.0 convolution_add_fusion.1
  41.6 1.0 copy.42
  43.6 1.3 fusion.44
  48.2 0.7 collective-permute-start.1
  49.0 5.3 %collective-permute-done.1 = bf16[384,192]{0,1:T(8,128)(2,1)S(1)} collective-permute-done((bf16[384,192]{0,1:T(8,128)(2,1)S(1)}, bf16[384,192]{0,1:T(8,128)(2,1)S(1)}, u32[]{:S(2)}, u32[]{:S(2)}) %collective-permute-start.1) | collective-permute-done | bytes 147488 | tf_op jit(solution)/shard_map/ppermute | solution.py:26
  54.3 5.4 %collective-permute-done.2 = bf16[384,192]{0,1:T(8,128)(2,1)S(1)} collective-permute-done((bf16[384,192]{0,1:T(8,128)(2,1)S(1)}, bf16[384,192]{0,1:T(8,128)(2,1)S(1)}, u32[]{:S(2)}, u32[]{:S(2)}) %collective-permute-start.2) | collective-permute-done | bytes 147488 | tf_op jit(solution)/shard_map/ppermute | solution.py:26
  59.8 6.1 %collective-permute-done.3 = bf16[384,192]{0,1:T(8,128)(2,1)S(1)} collective-permute-done((bf16[384,192]{0,1:T(8,128)(2,1)S(1)}, bf16[384,192]{0,1:T(8,128)(2,1)S(1)}, u32[]{:S(2)}, u32[]{:S(2)}) %collective-permute-start.3) | collective-permute-done | bytes 147488 | tf_op jit(solution)/shard_map/ppermute | solution.py:26
  66.0 5.4 %collective-permute-done.4 = bf16[384,192]{0,1:T(8,128)(2,1)S(1)} collective-permute-done((bf16[384,192]{0,1:T(8,128)(2,1)S(1)}, bf16[384,192]{0,1:T(8,128)(2,1)S(1)}, u32[]{:S(2)}, u32[]{:S(2)}) %collective-permute-start.4) | collective-permute-done | bytes 147488 | tf_op jit(solution)/shard_map/ppermute | solution.py:26
  71.4 5.4 %collective-permute-done.5 = bf16[384,192]{0,1:T(8,128)(2,1)S(1)} collective-permute-done((bf16[384,192]{0,1:T(8,128)(2,1)S(1)}, bf16[384,192]{0,1:T(8,128)(2,1)S(1)}, u32[]{:S(2)}, u32[]{:S(2)}) %collective-permute-start.5) | collective-permute-done | bytes 147488 | tf_op jit(solution)/shard_map/ppermute | solution.py:26
  76.9 8.2 %collective-permute-done.6 = bf16[384,192]{0,1:T(8,128)(2,1)S(1)} collective-permute-done((bf16[384,192]{0,1:T(8,128)(2,1)S(1)}, bf16[384,192]{0,1:T(8,128)(2,1)S(1)}, u32[]{:S(2)}, u32[]{:S(2)}) %collective-permute-start.6) | collective-permute-done | bytes 147488 | tf_op jit(solution)/shard_map/ppermute | solution.py:26
  85.1 0.8 gather_fusion
  86.0 2.7 convolution_add_fusion.3
  89.0 18.0 %all-gather.12.cloned.1.call-done = bf16[4096,512]{1,0:T(8,128)(2,1)} async-done(((bf16[512,512]{1,0:T(8,128)(2,1)}), bf16[4096,512]{1,0:T(8,128)(2,1)}) %all-gather.12.cloned.1.call-update) | async-done | bytes 4194320 | tf_op jit(solution)/shard_map/all_gather | solution.py:220
  107.1 3.4 constant_dynamic-slice_fusion
  110.6 5.7 %while.15 = (s32[]{:T(128)}, f32[1536]{0:T(1024)S(1)}, f32[1536]{0:T(1024)S(1)}, f32[1536,128]{1,0:T(8,128)S(1)}, s32[]{:T(128)}, /*index=5*/s32[8]{0:T(128)S(1)...) while((s32[]{:T(128)}, f32[1536]{0:T(1024)S(1)}, ...), condition=%wide.region_7.8_spmd.clone, body=%wide.region_3.7_spmd.clone.sunk | while | flops 419576320 | bytes 11870495 | solution.py:150
  110.8 2.2 fusion.75
  113.0 1.4 fusion.76
  114.5 1.8 convolution_add_fusion.5
  116.8 1.0 convolution_convert_fusion.1
  117.8 1.6 copy.43
  119.5 58.3 %reduce-scatter.7.cloned.1.call-done = bf16[384,512]{1,0:T(8,128)(2,1)} async-done(((bf16[1536,512]{1,0:T(8,128)(2,1)}), bf16[384,512]{1,0:T(8,128)(2,1)}) %reduce-scatter.7.cloned.1.call-update) | async-done | bytes 393232
  177.7 1.2 copy.44
  179.0 1.8 add_convert_fusion.1
  181.4 0.7 all-gather.20.cloned.1.call-update
  182.3 13.4 %collective-permute-done.7 = bf16[2240,192]{0,1:T(8,128)(2,1)S(1)} collective-permute-done((bf16[2240,192]{0,1:T(8,128)(2,1)S(1)}, bf16[2240,192]{0,1:T(8,128)(2,1)S(1)}, u32[]{:S(2)}, u32[]{:S(2)}) %collective-permute-start.7) | collective-permute-done | bytes 860192 | tf_op jit(solution)/shard_map/ppermute | solution.py:26
  195.6 13.4 %collective-permute-done.8 = bf16[2240,192]{0,1:T(8,128)(2,1)S(1)} collective-permute-done((bf16[2240,192]{0,1:T(8,128)(2,1)S(1)}, bf16[2240,192]{0,1:T(8,128)(2,1)S(1)}, u32[]{:S(2)}, u32[]{:S(2)}) %collective-permute-start.8) | collective-permute-done | bytes 860192 | tf_op jit(solution)/shard_map/ppermute | solution.py:26
  209.0 13.4 %collective-permute-done.9 = bf16[2240,192]{0,1:T(8,128)(2,1)S(1)} collective-permute-done((bf16[2240,192]{0,1:T(8,128)(2,1)S(1)}, bf16[2240,192]{0,1:T(8,128)(2,1)S(1)}, u32[]{:S(2)}, u32[]{:S(2)}) %collective-permute-start.9) | collective-permute-done | bytes 860192 | tf_op jit(solution)/shard_map/ppermute | solution.py:26
  222.4 1.0 bitcast_dynamic-update-slice_fusion.7
  223.4 21.8 %collective-permute-done.10 = bf16[2240,192]{0,1:T(8,128)(2,1)S(1)} collective-permute-done((bf16[2240,192]{0,1:T(8,128)(2,1)S(1)}, bf16[2240,192]{0,1:T(8,128)(2,1)S(1)}, u32[]{:S(2)}, u32[]{:S(2)}) %collective-permute-start.10) | collective-permute-done | bytes 860192 | tf_op jit(solution)/shard_map/ppermute | solution.py:26
  245.2 1.0 bitcast_dynamic-update-slice_fusion.6
  246.2 1.0 bitcast_dynamic-update-slice_fusion.5
  247.2 26.5 %collective-permute-done.11 = bf16[2240,192]{0,1:T(8,128)(2,1)S(1)} collective-permute-done((bf16[2240,192]{0,1:T(8,128)(2,1)S(1)}, bf16[2240,192]{0,1:T(8,128)(2,1)S(1)}, u32[]{:S(2)}, u32[]{:S(2)}) %collective-permute-start.11) | collective-permute-done | bytes 860192 | tf_op jit(solution)/shard_map/ppermute | solution.py:26
  273.7 1.0 bitcast_dynamic-update-slice_fusion.4
  274.6 1.1 bitcast_dynamic-update-slice_fusion.3
  275.7 11.3 %collective-permute-done.12 = bf16[2240,192]{0,1:T(8,128)(2,1)S(1)} collective-permute-done((bf16[2240,192]{0,1:T(8,128)(2,1)S(1)}, bf16[2240,192]{0,1:T(8,128)(2,1)S(1)}, u32[]{:S(2)}, u32[]{:S(2)}) %collective-permute-start.12) | collective-permute-done | bytes 860192 | tf_op jit(solution)/shard_map/ppermute | solution.py:26
  287.0 1.0 bitcast_dynamic-update-slice_fusion.2
  288.0 1.0 bitcast_dynamic-update-slice_fusion.1
  289.0 20.9 %collective-permute-done.13 = bf16[2240,192]{0,1:T(8,128)(2,1)S(1)} collective-permute-done((bf16[2240,192]{0,1:T(8,128)(2,1)S(1)}, bf16[2240,192]{0,1:T(8,128)(2,1)S(1)}, u32[]{:S(2)}, u32[]{:S(2)}) %collective-permute-start.13) | collective-permute-done | bytes 860192 | tf_op jit(solution)/shard_map/ppermute | solution.py:26
  309.9 1.0 bitcast_dynamic-update-slice_fusion
  310.9 7.4 %gather_fusion.1 = bf16[8,2240,192]{1,2,0:T(8,128)(2,1)} fusion(bf16[8,2240,192]{1,2,0:T(8,128)(2,1)} %bitcast_dynamic-update-slice_fusion, s32[1024]{0:T(1024)S(1)} %pad_clamp_fusion.1), kind=kCustom, calls=%fused_computation.1 | custom fusion | bytes 13762592 | tf_op jit(solution)/shard_map/gather | solution.py:30
  318.3 1.9 fusion.20
  320.2 9.6 %fusion.28 = f32[512,2240]{0,1:T(8,128)} fusion(bf16[1536,2240]{1,0:T(8,128)(2,1)} %all-gather.18.cloned.1.call-done, bf16[512,1536]{1,0:T(8,128)(2,1)} %all-gather.16.cloned.1.call-done, f32[1536]{0:T(1024)S(1)} %convert_element_type.121, f32[512]{0:T(512)S(1)} %add_rsqrt_fusion.1), kind=kOutput, calls=%fused_computation.62 | convolution fusion | flops 3526361088 | bytes 13049856 | tf_op jit(solution)/shard_map/dot_general | solution.py:64
  329.8 4.1 all-gather.20.cloned.1.call-done
  333.9 15.9 %convolution_convert_fusion = bf16[512,1536]{1,0:T(8,128)(2,1)} fusion(bf16[2240,1536]{0,1:T(8,128)(2,1)} %bitcast.89, bf16[1536,2240]{1,0:T(8,128)(2,1)} %all-gather.20.cloned.1.call-done, f32[512,2240]{0,1:T(8,128)} %fusion.28, bf16[512,1536]{1,0:T(8,128)(2,1)S(1)} %copy-done.2, f32[1536]{0:T(1024)S(1)} %convert_element_type.121, f32[512]{0:T(512)S(1)} %add_rsqrt_fusion.1), kind=kOutput, calls=%fused_computation.42 | convolution fusion | flops 7057244160 | bytes 21504000 | tf_op jit(solution)/shard_map/dot_general | solution.py:78
  349.8 2.7 copy.45
  352.6 35.4 %reduce-scatter.9.cloned.1.call-done = bf16[384,512]{1,0:T(8,128)(2,1)} async-done(((bf16[1536,512]{1,0:T(8,128)(2,1)}), bf16[384,512]{1,0:T(8,128)(2,1)}) %reduce-scatter.9.cloned.1.call-update) | async-done | bytes 393232
  388.0 1.2 copy.46
  389.2 0.8 add_convert_fusion
  392.6 2.0 gather_fusion.2
  394.6 0.9 select_select_fusion
  395.5 30.9 %all-gather.22.cloned.1.call-done = bf16[512,1536]{1,0:T(8,128)(2,1)} async-done(((bf16[512,384]{1,0:T(8,128)(2,1)}), bf16[512,1536]{1,0:T(8,128)(2,1)}) %all-gather.22.cloned.1.call-update) | async-done | bytes 1572880 | tf_op jit(solution)/shard_map/all_gather | solution.py:96
  426.3 1.8 fusion.23
  428.1 24.6 %all-gather.26.cloned.1.call-done = bf16[1536,512]{1,0:T(8,128)(2,1)} async-done(((bf16[192,512]{1,0:T(8,128)(2,1)}), bf16[1536,512]{1,0:T(8,128)(2,1)}) %all-gather.26.cloned.1.call-update) | async-done | bytes 1572880 | tf_op jit(solution)/shard_map/all_gather | solution.py:71
  452.7 2.9 fusion.30
  455.6 0.7 fusion.35
  456.3 22.4 %all-gather.24.cloned.1.call-done = bf16[1536,384]{1,0:T(8,128)(2,1)} async-done(((bf16[192,384]{1,0:T(8,128)(2,1)}), bf16[1536,384]{1,0:T(8,128)(2,1)}) %all-gather.24.cloned.1.call-update) | async-done | bytes 1179664 | tf_op jit(solution)/shard_map/all_gather | solution.py:66
  478.7 3.0 fusion.26
  481.8 1.1 copy.77
  (121 shorter events, 7.8 us)
Async XLA Ops:
  7.2 31.1 %all-gather.10.cloned.1.call-start = ((), (), s32[]{:S(2)}) async-start(), calls=%async_computation.2 | async-start | bytes 1769472 | tf_op jit(solution)/shard_map/all_gather | solution.py:71
  7.9 78.1 %all-gather.14.cloned.1.call-start = ((), (), s32[]{:S(2)}) async-start(), calls=%async_computation.4 | async-start | bytes 1327104 | tf_op jit(solution)/shard_map/all_gather | solution.py:66
  8.6 98.4 %all-gather.12.cloned.1.call-start = ((), (), s32[]{:S(2)}) async-start(), calls=%async_computation.3 | async-start | bytes 4718592 | tf_op jit(solution)/shard_map/all_gather | solution.py:220
  41.3 1.4 copy-start.4
  41.3 1.7 copy-start.5
  41.3 2.2 copy-start.9
  41.3 6.2 %copy-start.10 = (bf16[384]{0:T(512)(128)(2,1)S(1)}, bf16[384]{0:T(512)(128)(2,1)}, u32[]{:S(2)}) copy-start(bf16[384]{0:T(512)(128)(2,1)} %param.29) | copy-start | bytes 2308
  42.7 135.1 %reduce-scatter.7.cloned.1.call-start = ((), (), s32[]{:S(2)}) async-start(), calls=%async_computation.11 | async-start | bytes 1966080
  42.7 5.5 %collective-permute-start = (bf16[384,192]{0,1:T(8,128)(2,1)S(1)}, bf16[384,192]{0,1:T(8,128)(2,1)S(1)}, u32[]{:S(2)}, u32[]{:S(2)}) collective-permute-start(bf16[384,192]{0,1:T(8,128)(2,1)S(1)} %copy-done.4), channel_id=1, source_target_pairs={{0,4},{4,8},{8,12},{12,16},{16,20},{20,24},{24,28},{28,0},{1,5},{5... | collective-permute-start | bytes 442376 | tf_op jit(solution)/shard_map/ppermute | solution.py:26
  48.2 6.1 %collective-permute-start.1 = (bf16[384,192]{0,1:T(8,128)(2,1)S(1)}, bf16[384,192]{0,1:T(8,128)(2,1)S(1)}, u32[]{:S(2)}, u32[]{:S(2)}) collective-permute-start(bf16[384,192]{0,1:T(8,128)(2,1)S(1)} %collective-permute-done), channel_id=1, source_target_pairs={{0,4},{4,8},{8,12},{12,16},{16,20},{20,24},{24,28},{28,0},{1,5},{5... | collective-permute-start | bytes 442376 | tf_op jit(solution)/shard_map/ppermute | solution.py:26
  54.3 5.5 %collective-permute-start.2 = (bf16[384,192]{0,1:T(8,128)(2,1)S(1)}, bf16[384,192]{0,1:T(8,128)(2,1)S(1)}, u32[]{:S(2)}, u32[]{:S(2)}) collective-permute-start(bf16[384,192]{0,1:T(8,128)(2,1)S(1)} %collective-permute-done.1), channel_id=1, source_target_pairs={{0,4},{4,8},{8,12},{12,16},{16,20},{20,24},{24,28},{28,0},{1,5},{5... | collective-permute-start | bytes 442376 | tf_op jit(solution)/shard_map/ppermute | solution.py:26
  59.8 6.2 %collective-permute-start.3 = (bf16[384,192]{0,1:T(8,128)(2,1)S(1)}, bf16[384,192]{0,1:T(8,128)(2,1)S(1)}, u32[]{:S(2)}, u32[]{:S(2)}) collective-permute-start(bf16[384,192]{0,1:T(8,128)(2,1)S(1)} %collective-permute-done.2), channel_id=1, source_target_pairs={{0,4},{4,8},{8,12},{12,16},{16,20},{20,24},{24,28},{28,0},{1,5},{5... | collective-permute-start | bytes 442376 | tf_op jit(solution)/shard_map/ppermute | solution.py:26
  65.9 5.5 %collective-permute-start.4 = (bf16[384,192]{0,1:T(8,128)(2,1)S(1)}, bf16[384,192]{0,1:T(8,128)(2,1)S(1)}, u32[]{:S(2)}, u32[]{:S(2)}) collective-permute-start(bf16[384,192]{0,1:T(8,128)(2,1)S(1)} %collective-permute-done.3), channel_id=1, source_target_pairs={{0,4},{4,8},{8,12},{12,16},{16,20},{20,24},{24,28},{28,0},{1,5},{5... | collective-permute-start | bytes 442376 | tf_op jit(solution)/shard_map/ppermute | solution.py:26
  71.4 5.5 %collective-permute-start.5 = (bf16[384,192]{0,1:T(8,128)(2,1)S(1)}, bf16[384,192]{0,1:T(8,128)(2,1)S(1)}, u32[]{:S(2)}, u32[]{:S(2)}) collective-permute-start(bf16[384,192]{0,1:T(8,128)(2,1)S(1)} %collective-permute-done.4), channel_id=1, source_target_pairs={{0,4},{4,8},{8,12},{12,16},{16,20},{20,24},{24,28},{28,0},{1,5},{5... | collective-permute-start | bytes 442376 | tf_op jit(solution)/shard_map/ppermute | solution.py:26
  76.9 8.2 %collective-permute-start.6 = (bf16[384,192]{0,1:T(8,128)(2,1)S(1)}, bf16[384,192]{0,1:T(8,128)(2,1)S(1)}, u32[]{:S(2)}, u32[]{:S(2)}) collective-permute-start(bf16[384,192]{0,1:T(8,128)(2,1)S(1)} %collective-permute-done.5), channel_id=1, source_target_pairs={{0,4},{4,8},{8,12},{12,16},{16,20},{20,24},{24,28},{28,0},{1,5},{5... | collective-permute-start | bytes 442376 | tf_op jit(solution)/shard_map/ppermute | solution.py:26
  119.4 62.8 %copy-start.3 = (bf16[2240,192]{0,1:T(8,128)(2,1)S(1)}, bf16[2240,192]{0,1:T(8,128)(2,1)}, u32[]{:S(2)}) copy-start(bf16[2240,192]{0,1:T(8,128)(2,1)} %param.36) | copy-start | bytes 2580484
  119.4 103.0 %copy-start.7 = (bf16[1536]{0:T(1024)(128)(2,1)S(1)}, bf16[1536]{0:T(1024)(128)(2,1)}, u32[]{:S(2)}) copy-start(bf16[1536]{0:T(1024)(128)(2,1)} %param.33) | copy-start | bytes 9220
  119.4 198.8 %all-gather.16.cloned.1.call-start = ((), (), s32[]{:S(2)}) async-start(), calls=%async_computation.5 | async-start | bytes 1966080 | tf_op jit(solution)/shard_map/all_gather | solution.py:96
  180.8 139.4 %all-gather.18.cloned.1.call-start = ((), (), s32[]{:S(2)}) async-start(), calls=%async_computation.6 | async-start | bytes 7962624 | tf_op jit(solution)/shard_map/all_gather | solution.py:66
  181.4 152.5 %all-gather.20.cloned.1.call-start = ((), (), s32[]{:S(2)}) async-start(), calls=%async_computation.7 | async-start | bytes 7962624 | tf_op jit(solution)/shard_map/all_gather | solution.py:71
  182.2 205.9 %reduce-scatter.9.cloned.1.call-start = ((), (), s32[]{:S(2)}) async-start(), calls=%async_computation.12 | async-start | bytes 1966080
  182.2 13.4 %collective-permute-start.7 = (bf16[2240,192]{0,1:T(8,128)(2,1)S(1)}, bf16[2240,192]{0,1:T(8,128)(2,1)S(1)}, u32[]{:S(2)}, u32[]{:S(2)}) collective-permute-start(bf16[2240,192]{0,1:T(8,128)(2,1)S(1)} %copy-done.3), channel_id=1, source_target_pairs={{0,4},{4,8},{8,12},{12,16},{16,20},{20,24},{24,28},{28,0},{1,5},{5... | collective-permute-start | bytes 2580488 | tf_op jit(solution)/shard_map/ppermute | solution.py:26
  195.6 13.4 %collective-permute-start.8 = (bf16[2240,192]{0,1:T(8,128)(2,1)S(1)}, bf16[2240,192]{0,1:T(8,128)(2,1)S(1)}, u32[]{:S(2)}, u32[]{:S(2)}) collective-permute-start(bf16[2240,192]{0,1:T(8,128)(2,1)S(1)} %collective-permute-done.7), channel_id=1, source_target_pairs={{0,4},{4,8},{8,12},{12,16},{16,20},{20,24},{24,28},{28,0},{1,5},{5... | collective-permute-start | bytes 2580488 | tf_op jit(solution)/shard_map/ppermute | solution.py:26
  209.0 13.4 %collective-permute-start.9 = (bf16[2240,192]{0,1:T(8,128)(2,1)S(1)}, bf16[2240,192]{0,1:T(8,128)(2,1)S(1)}, u32[]{:S(2)}, u32[]{:S(2)}) collective-permute-start(bf16[2240,192]{0,1:T(8,128)(2,1)S(1)} %collective-permute-done.8), channel_id=1, source_target_pairs={{0,4},{4,8},{8,12},{12,16},{16,20},{20,24},{24,28},{28,0},{1,5},{5... | collective-permute-start | bytes 2580488 | tf_op jit(solution)/shard_map/ppermute | solution.py:26
  222.4 22.8 %collective-permute-start.10 = (bf16[2240,192]{0,1:T(8,128)(2,1)S(1)}, bf16[2240,192]{0,1:T(8,128)(2,1)S(1)}, u32[]{:S(2)}, u32[]{:S(2)}) collective-permute-start(bf16[2240,192]{0,1:T(8,128)(2,1)S(1)} %collective-permute-done.9), channel_id=1, source_target_pairs={{0,4},{4,8},{8,12},{12,16},{16,20},{20,24},{24,28},{28,0},{1,5},{5... | collective-permute-start | bytes 2580488 | tf_op jit(solution)/shard_map/ppermute | solution.py:26
  245.2 28.4 %collective-permute-start.11 = (bf16[2240,192]{0,1:T(8,128)(2,1)S(1)}, bf16[2240,192]{0,1:T(8,128)(2,1)S(1)}, u32[]{:S(2)}, u32[]{:S(2)}) collective-permute-start(bf16[2240,192]{0,1:T(8,128)(2,1)S(1)} %collective-permute-done.10), channel_id=1, source_target_pairs={{0,4},{4,8},{8,12},{12,16},{16,20},{20,24},{24,28},{28,0},{1,5},{5... | collective-permute-start | bytes 2580488 | tf_op jit(solution)/shard_map/ppermute | solution.py:26
  273.7 13.4 %collective-permute-start.12 = (bf16[2240,192]{0,1:T(8,128)(2,1)S(1)}, bf16[2240,192]{0,1:T(8,128)(2,1)S(1)}, u32[]{:S(2)}, u32[]{:S(2)}) collective-permute-start(bf16[2240,192]{0,1:T(8,128)(2,1)S(1)} %collective-permute-done.11), channel_id=1, source_target_pairs={{0,4},{4,8},{8,12},{12,16},{16,20},{20,24},{24,28},{28,0},{1,5},{5... | collective-permute-start | bytes 2580488 | tf_op jit(solution)/shard_map/ppermute | solution.py:26
  287.0 22.8 %collective-permute-start.13 = (bf16[2240,192]{0,1:T(8,128)(2,1)S(1)}, bf16[2240,192]{0,1:T(8,128)(2,1)S(1)}, u32[]{:S(2)}, u32[]{:S(2)}) collective-permute-start(bf16[2240,192]{0,1:T(8,128)(2,1)S(1)} %collective-permute-done.12), channel_id=1, source_target_pairs={{0,4},{4,8},{8,12},{12,16},{16,20},{20,24},{24,28},{28,0},{1,5},{5... | collective-permute-start | bytes 2580488 | tf_op jit(solution)/shard_map/ppermute | solution.py:26
  320.2 13.7 %copy-start.2 = (bf16[512,1536]{1,0:T(8,128)(2,1)S(1)}, bf16[512,1536]{1,0:T(8,128)(2,1)}, u32[]{:S(2)}) copy-start(bf16[512,1536]{1,0:T(8,128)(2,1)} %all-gather.16.cloned.1.call-done) | copy-start | bytes 4718596
  349.8 41.6 %copy-start.6 = (s32[8,16]{1,0:T(8,128)S(1)}, s32[8,16]{1,0:T(8,128)}, u32[]{:S(2)}) copy-start(s32[8,16]{1,0:T(8,128)} %param.26) | copy-start | bytes 1540
  349.8 42.0 %copy-start.12 = (s32[8]{0:T(128)S(1)}, s32[8]{0:T(128)}, u32[]{:S(2)}) copy-start(s32[8]{0:T(128)} %param.24) | copy-start | bytes 100
  349.8 42.2 %copy-start.8 = (bf16[1536]{0:T(1024)(128)(2,1)S(1)}, bf16[1536]{0:T(1024)(128)(2,1)}, u32[]{:S(2)}) copy-start(bf16[1536]{0:T(1024)(128)(2,1)} %param.37) | copy-start | bytes 9220
  349.8 42.2 %copy-start.13 = (bf16[512]{0:T(512)(128)(2,1)S(1)}, bf16[512]{0:T(512)(128)(2,1)}, u32[]{:S(2)}) copy-start(bf16[512]{0:T(512)(128)(2,1)} %param.41) | copy-start | bytes 3076
  349.8 42.3 %copy-start.11 = (bf16[384]{0:T(512)(128)(2,1)S(1)}, bf16[384]{0:T(512)(128)(2,1)}, u32[]{:S(2)}) copy-start(bf16[384]{0:T(512)(128)(2,1)} %param.39) | copy-start | bytes 2308
  349.8 42.7 %copy-start.1 = (bf16[4096,128]{1,0:T(8,128)(2,1)S(1)}, bf16[4096,128]{1,0:T(8,128)(2,1)}, u32[]{:S(2)}) copy-start(bf16[4096,128]{1,0:T(8,128)(2,1)} %get-tuple-element.123) | copy-start | bytes 3145732
  352.6 73.8 %all-gather.22.cloned.1.call-start = ((), (), s32[]{:S(2)}) async-start(), calls=%async_computation.8 | async-start | bytes 1966080 | tf_op jit(solution)/shard_map/all_gather | solution.py:96
  390.1 62.6 %all-gather.26.cloned.1.call-start = ((), (), s32[]{:S(2)}) async-start(), calls=%async_computation.10 | async-start | bytes 1769472 | tf_op jit(solution)/shard_map/all_gather | solution.py:71
  390.7 88.0 %all-gather.24.cloned.1.call-start = ((), (), s32[]{:S(2)}) async-start(), calls=%async_computation.9 | async-start | bytes 1327104 | tf_op jit(solution)/shard_map/all_gather | solution.py:66
  428.1 50.6 %copy-start = (bf16[512,1536]{1,0:T(8,128)(2,1)S(1)}, bf16[512,1536]{1,0:T(8,128)(2,1)}, u32[]{:S(2)}) copy-start(bf16[512,1536]{1,0:T(8,128)(2,1)} %all-gather.22.cloned.1.call-done) | copy-start | bytes 4718596
Sparse Core Ops, SparseCore 0:
  9.9 28.3 all-gather.9
  40.2 25.0 all-gather.13
  67.8 39.2 all-gather.11
  119.5 58.1 reduce-scatter.6
  180.9 36.0 all-gather.15
  218.8 60.6 all-gather.17
  281.4 52.4 all-gather.19
  352.7 35.2 reduce-scatter.8
  390.2 36.0 all-gather.21
  428.1 24.6 all-gather.25
  454.6 24.0 all-gather.23
